TPU v7x, 32 devices: a whole 2x2x4 slice. The times are simulated.
32 devices in a mesh: sec: 2 (over y), blk: 16 (over z, x, core).
Axes of the slice: x: 2, y: 2, z: 4, core: 2. Of those that a mesh axis runs over, the one named last changes fastest.
Arguments:
- wave_speed: float32 [2, 125, 4096], P('sec', None, 'blk'), may hold values from 0.5 to 2
- inverse_mass: float32 [2, 125, 4096], P('sec', None, 'blk'), may hold values from 0.5 to 2
- source_field: float32 [2, 125, 4096], P('sec', None, 'blk'), may hold values from -4 to 4
- source_time: float32 [2, 12], P('sec'), may hold values from -4 to 4
- face_links: int32 [2, 3, 2048], P('sec', None, 'blk'), may hold values from 0 to 255, as said below
- coupling_links: int32 [5, 8192], P(None, 'blk'), may hold values from -1 to 255, as said below
Outputs:
- adjoint_now: float32 [2, 125, 4096], P('sec', None, 'blk')
- adjoint_before: float32 [2, 125, 4096], P('sec', None, 'blk')
Inputs may be any that keep to these rules, and one draw needn't show every extreme that they name: `face_links`: in each section record k of block b and record k of its peer name each other; the peer is b XOR 2^j for a bit j that depends on the section and k only, and equals b for unlinked records, which are the trailing ones. A block's records name distinct elements. A block has at most 16 records with one peer and exactly 16 with some peer. `coupling_links`: owner -1 marks unused points, which are the trailing points of a block. A box block has at most 4 points with one owner, and every box block has exactly 4 points with one common owner.
All inputs are finite; a program needn't handle non-finite values.
Results may differ from a plain program's by a relative error of at most 0.0001.
Values sent between devices are 32-bit elements; how exact they have to be, the bound alone decides.
No kernel may reach another device: no remote copies, remote signals or barrier semaphores. Data moves between devices by JAX's collectives and lax.ppermute only.
A program may use at most 64 MiB of HBM per device.

v0:
```python
import jax
import jax.numpy as jnp
import numpy as np
from jax import lax
from jax.sharding import PartitionSpec as P

CAPC = 4
STEPS = 12
DT_SQUARED = 0.05
PENALTY = 10.0


def partner_2(value, axis, stride):
    return lax.ppermute(value, axis, [(i, i ^ 1 << stride) for i in range(lax.axis_size(axis))])


def node_tables():
    abscissae = np.array([-1.0, -np.sqrt(3.0 / 7.0), 0.0, np.sqrt(3.0 / 7.0), 1.0])
    weights = np.array([0.1, 49.0 / 90.0, 32.0 / 45.0, 49.0 / 90.0, 0.1])
    legendre = (35.0 * abscissae**4 - 30.0 * abscissae**2 + 3.0) / 8.0
    derivative = np.zeros((5, 5))
    for i in range(5):
        for j in range(5):
            if i != j:
                derivative[i, j] = legendre[i] / (legendre[j] * (abscissae[i] - abscissae[j]))
    derivative[0, 0] = -2.5
    derivative[4, 4] = 2.5
    identity = np.eye(5)
    operator = np.concatenate(
        [
            np.kron(np.kron(derivative, identity), identity),
            np.kron(np.kron(identity, derivative), identity),
            np.kron(np.kron(identity, identity), derivative),
        ],
        axis=0,
    )
    weight_cube = weights[:, None, None] * weights[None, :, None] * weights[None, None, :]
    lattice = np.arange(125).reshape(5, 5, 5)
    face_nodes = np.stack(
        [
            lattice[0].ravel(),
            lattice[4].ravel(),
            lattice[:, 0].ravel(),
            lattice[:, 4].ravel(),
            lattice[:, :, 0].ravel(),
            lattice[:, :, 4].ravel(),
        ]
    )
    return (
        operator.astype(np.float32),
        weight_cube.reshape(125, 1).astype(np.float32),
        face_nodes.astype(np.int32),
    )


def stiffness(field_in, speed_sq, operator, weight_cube):
    columns = field_in.shape[-1]
    scaling = weight_cube * speed_sq
    grads = jnp.dot(
        operator, field_in, precision=lax.Precision.HIGHEST, preferred_element_type=jnp.float32
    )
    scaled = (grads.reshape(3, 125, columns) * scaling[None]).reshape(375, columns)
    return jnp.dot(
        operator.T, scaled, precision=lax.Precision.HIGHEST, preferred_element_type=jnp.float32
    )


def body(wave_speed, inverse_mass, source_field, source_time, face_links, coupling_links):
    operator_np, weight_np, faces_np = node_tables()
    operator = jnp.asarray(operator_np)
    weight_cube = jnp.asarray(weight_np)
    picker_np = np.zeros((150, 125), np.float32)
    for side_number in range(6):
        for node_number in range(25):
            picker_np[side_number * 25 + node_number, faces_np[side_number, node_number]] = 1.0
    picker = jnp.asarray(picker_np)
    spreader = jnp.asarray(picker_np.T.copy())
    speed_sq = wave_speed[0]
    inverse = inverse_mass[0]
    forcing = source_field[0]
    timing = source_time[0]
    element = face_links[0, 0]
    face_side = face_links[0, 1]
    face_peer = face_links[0, 2]
    blocks = lax.axis_size("blk")
    bit_count = blocks.bit_length() - 1
    myself = lax.axis_index("blk")
    is_box = lax.axis_index("sec") == 0
    records = element.shape[0]
    per_peer = records // 8
    ordinal = jnp.arange(records)
    linked = face_peer != myself
    side_mask = face_side[None, None, :] == jnp.arange(6, dtype=jnp.int32)[:, None, None]
    earlier = ordinal[None, :] < ordinal[:, None]
    face_slot = jnp.sum(
        ((face_peer[:, None] == face_peer[None, :]) & earlier).astype(jnp.int32), axis=1
    )
    offset_bits = jnp.bitwise_xor(face_peer, myself)
    bit_index = jnp.zeros((records,), jnp.int32)
    for bit_number in range(bit_count):
        bit_index = bit_index + bit_number * (offset_bits == 1 << bit_number).astype(jnp.int32)
    pair_column = jnp.where(linked, bit_index * per_peer + face_slot, 0)
    point_element = coupling_links[0]
    point_node = coupling_links[1]
    point_owner = coupling_links[2]
    target_element = coupling_links[3]
    target_node = coupling_links[4]
    in_use = point_owner >= 0
    owner_safe = jnp.maximum(point_owner, 0)
    point_ordinal = jnp.arange(point_owner.shape[0])
    point_earlier = point_ordinal[None, :] < point_ordinal[:, None]
    point_slot = jnp.sum(
        ((point_owner[:, None] == point_owner[None, :]) & point_earlier).astype(jnp.int32), axis=1
    )
    point_column = jnp.where(in_use, point_slot * blocks + owner_safe, 0)
    slot_total = CAPC * blocks
    outbound = jnp.zeros((3, slot_total), jnp.int32)
    outbound = outbound.at[0, point_column].add(jnp.where(in_use, target_element, 0))
    outbound = outbound.at[1, point_column].add(jnp.where(in_use, target_node, 0))
    outbound = outbound.at[2, point_column].add(in_use.astype(jnp.int32))
    inbound = lax.all_to_all(
        outbound.reshape(3, CAPC, blocks), "blk", split_axis=2, concat_axis=2, tiled=True
    ).reshape(3, slot_total)
    remote_element = inbound[0]
    remote_node = inbound[1]
    remote_flag = inbound[2].astype(jnp.float32)
    target_rows = jnp.concatenate([point_node, remote_node])
    target_cols = jnp.concatenate([point_element, remote_element])
    current = jnp.zeros(speed_sq.shape, jnp.float32)
    previous = jnp.zeros(speed_sq.shape, jnp.float32)
    for moment in range(STEPS):
        internal = stiffness(current, speed_sq, operator, weight_cube)
        stacked = jnp.dot(
            picker,
            internal[:, element],
            precision=lax.Precision.HIGHEST,
            preferred_element_type=jnp.float32,
        ).reshape(6, 25, records)
        payload = jnp.sum(jnp.where(side_mask, stacked, 0.0), axis=0)
        payload = jnp.where(linked[None, :], payload, 0.0)
        outgoing = (
            jnp.zeros((25, bit_count * per_peer), jnp.float32).at[:, pair_column].add(payload)
        )
        arrived = []
        for bit_number in range(bit_count):
            piece = outgoing[:, bit_number * per_peer : (bit_number + 1) * per_peer]
            arrived.append(partner_2(piece, "blk", bit_number))
        partner = jnp.concatenate(arrived, axis=1)[:, pair_column]
        partner = jnp.where(linked[None, :], partner, 0.0)
        masked = jnp.where(side_mask, partner[None], 0.0).reshape(150, records)
        assembled = internal.at[:, element].add(
            jnp.dot(
                spreader,
                masked,
                precision=lax.Precision.HIGHEST,
                preferred_element_type=jnp.float32,
            )
        )
        velocity = current - previous
        traction = assembled[point_node, point_element]
        box_send = (
            jnp.zeros((slot_total,), jnp.float32)
            .at[point_column]
            .add(jnp.where(in_use, traction, 0.0))
        )
        global_send = velocity[remote_node, remote_element] * remote_flag
        dispatch = jnp.where(is_box, box_send, global_send).reshape(CAPC, blocks)
        crossed = partner_2(dispatch, "sec", 0)
        received = lax.all_to_all(crossed, "blk", split_axis=1, concat_axis=1, tiled=True)
        received = received.reshape(slot_total)
        remote_velocity = received[point_column]
        box_terms = jnp.where(
            in_use, PENALTY * (remote_velocity - velocity[point_node, point_element]), 0.0
        )
        values = jnp.concatenate(
            [jnp.where(is_box, box_terms, 0.0), jnp.where(is_box, 0.0, received * remote_flag)]
        )
        driving = timing[moment] * forcing - assembled
        driving = driving.at[target_rows, target_cols].add(values)
        advanced = 2.0 * current - previous + DT_SQUARED * inverse * driving
        previous = current
        current = advanced
    return (current[None], previous[None])


def solution(mesh):
    in_specs = (
        P("sec", None, "blk"),
        P("sec", None, "blk"),
        P("sec", None, "blk"),
        P("sec", None),
        P("sec", None, "blk"),
        P(None, "blk"),
    )
    out_specs = (P("sec", None, "blk"), P("sec", None, "blk"))
    return jax.shard_map(body, mesh=mesh, in_specs=in_specs, out_specs=out_specs, check_vma=False)
```

profile of v0, /device:TPU:0, one launch (start us, length us, event | category | flops | bytes accessed | tf_op | source)
XLA Modules:
  0.0 1408.7 jit_solution(6198110718570769417)
XLA Ops:
  24.5 22.8 %scatter_fusion.1 = s32[3,64]{1,0:T(4,128)S(1)} fusion(s32[3,64]{1,0:T(4,128)S(1)} %broadcast_in_dim.578, s32[512]{0:T(512)S(1)} %bitcast.1117, s32[512]{0:T(512)S(1)} %get-tuple-element.946), kind=kCustom, calls=%fused_computation.62 | custom fusion | flops 512 | bytes 10240 | tf_op jit(solution)/shard_map/scatter-add | solution.py:118
  47.3 22.8 %scatter_fusion.2 = s32[3,64]{1,0:T(4,128)S(1)} fusion(s32[3,64]{1,0:T(4,128)S(1)} %scatter_fusion.1, s32[512]{0:T(512)S(1)} %bitcast.1116, s32[512]{0:T(512)S(1)} %get-tuple-element.945), kind=kCustom, calls=%fused_computation.63 | custom fusion | flops 512 | bytes 10240 | tf_op jit(solution)/shard_map/scatter-add | solution.py:119
  70.0 22.8 %scatter_fusion.3 = s32[3,64]{1,0:T(4,128)S(1)} fusion(s32[3,64]{1,0:T(4,128)S(1)} %scatter_fusion.2, s32[512]{0:T(512)S(1)} %bitcast.1115, s32[512]{0:T(512)S(1)} %convert_element_type.31), kind=kCustom, calls=%fused_computation.64 | custom fusion | flops 512 | bytes 10240 | tf_op jit(solution)/shard_map/scatter-add | solution.py:120
  112.4 6.2 all-to-all-start.1
  118.6 6.3 all-to-all-done.1
  128.0 40.1 %fusion.83 = (f32[512]{0:T(512)S(1)}, pred[512]{0:T(512)(128)(4,1)S(1)}, pred[512]{0:T(512)(128)(4,1)S(1)}, pred[512]{0:T(512)(128)(4,1)S(1)}, pred[512]{0:T(512...) fusion(pred[512]{0:T(512)(128)(4,1)S(1)} %get-tuple-element.99,, ...), kind=kLoop, calls=%fused_computation.341 | loop fusion | flops 66560 | bytes 39169 | tf_op jit(solution)/shard_map/jit(_where)/select_n | solution.py:176
  168.1 30.1 %scatter_fusion.4 = f32[125,256]{1,0:T(8,128)S(1)} fusion(f32[125,256]{1,0:T(8,128)S(1)} %copy.421, s32[576]{0:T(1024)S(1)} %fusion.42, f32[576]{0:T(1024)S(1)} %pad_maximum_fusion.12), kind=kCustom, calls=%fused_computation.66 | custom fusion | flops 576 | bytes 11520 | tf_op jit(solution)/shard_map/scatter-add | solution.py:179
  238.2 40.1 %fusion.80 = f32[512]{0:T(512)S(1)} fusion(pred[512]{0:T(512)(128)(4,1)S(1)} %get-tuple-element.99, f32[512]{0:T(512)S(1)} %gather_fusion.9, pred[512]{0:T(512)(128)(4,1)S(1)} %get-tuple-element.97, pred[512]{0:T(512)(128)(4,1)S(1)} %get-tuple-element.96, pred[512]{0:T(512)(128)(4,1)S(1)} %get-tuple-element.95, pred[512]{0:T(512)(128)(4,1)S(1)} %get-tuple-element.94, ...), kind=kLoop, calls=%fused_computation.337 | loop fusion | flops 34304 | bytes 37121 | tf_op jit(solution)/shard_map/jit(_where)/select_n | solution.py:176
  278.3 30.1 %scatter_fusion.6 = f32[125,256]{1,0:T(8,128)S(1)} fusion(f32[125,256]{1,0:T(8,128)S(1)} %copy.429, s32[576]{0:T(1024)S(1)} %fusion.42, f32[576]{0:T(1024)S(1)} %pad_maximum_fusion.13), kind=kCustom, calls=%fused_computation.70 | custom fusion | flops 576 | bytes 11520 | tf_op jit(solution)/shard_map/scatter-add | solution.py:179
  339.2 5.6 all-to-all-done.3
  347.8 40.0 %fusion.77 = f32[512]{0:T(512)S(1)} fusion(pred[512]{0:T(512)(128)(4,1)S(1)} %get-tuple-element.99, f32[512]{0:T(512)S(1)} %gather_fusion.14, pred[512]{0:T(512)(128)(4,1)S(1)} %get-tuple-element.97, pred[512]{0:T(512)(128)(4,1)S(1)} %get-tuple-element.96, pred[512]{0:T(512)(128)(4,1)S(1)} %get-tuple-element.95, pred[512]{0:T(512)(128)(4,1)S(1)} %get-tuple-element.94, ...), kind=kLoop, calls=%fused_computation.333 | loop fusion | flops 34304 | bytes 37121 | tf_op jit(solution)/shard_map/jit(_where)/select_n | solution.py:176
  387.9 30.1 %scatter_fusion.8 = f32[125,256]{1,0:T(8,128)S(1)} fusion(f32[125,256]{1,0:T(8,128)S(1)} %copy.437, s32[576]{0:T(1024)S(1)} %fusion.42, f32[576]{0:T(1024)S(1)} %pad_maximum_fusion.14), kind=kCustom, calls=%fused_computation.74 | custom fusion | flops 576 | bytes 11520 | tf_op jit(solution)/shard_map/scatter-add | solution.py:179
  458.2 40.1 %fusion.74 = f32[512]{0:T(512)S(1)} fusion(pred[512]{0:T(512)(128)(4,1)S(1)} %get-tuple-element.99, f32[512]{0:T(512)S(1)} %gather_fusion.19, pred[512]{0:T(512)(128)(4,1)S(1)} %get-tuple-element.97, pred[512]{0:T(512)(128)(4,1)S(1)} %get-tuple-element.96, pred[512]{0:T(512)(128)(4,1)S(1)} %get-tuple-element.95, pred[512]{0:T(512)(128)(4,1)S(1)} %get-tuple-element.94, ...), kind=kLoop, calls=%fused_computation.329 | loop fusion | flops 34304 | bytes 37121 | tf_op jit(solution)/shard_map/jit(_where)/select_n | solution.py:176
  498.3 30.1 %scatter_fusion.10 = f32[125,256]{1,0:T(8,128)S(1)} fusion(f32[125,256]{1,0:T(8,128)S(1)} %copy.445, s32[576]{0:T(1024)S(1)} %fusion.42, f32[576]{0:T(1024)S(1)} %pad_maximum_fusion.15), kind=kCustom, calls=%fused_computation.78 | custom fusion | flops 576 | bytes 11520 | tf_op jit(solution)/shard_map/scatter-add | solution.py:179
  558.7 5.6 all-to-all-done.5
  567.4 39.9 %fusion.71 = f32[512]{0:T(512)S(1)} fusion(pred[512]{0:T(512)(128)(4,1)S(1)} %get-tuple-element.99, f32[512]{0:T(512)S(1)} %gather_fusion.24, pred[512]{0:T(512)(128)(4,1)S(1)} %get-tuple-element.97, pred[512]{0:T(512)(128)(4,1)S(1)} %get-tuple-element.96, pred[512]{0:T(512)(128)(4,1)S(1)} %get-tuple-element.95, pred[512]{0:T(512)(128)(4,1)S(1)} %get-tuple-element.94, ...), kind=kLoop, calls=%fused_computation.325 | loop fusion | flops 34304 | bytes 37121 | tf_op jit(solution)/shard_map/jit(_where)/select_n | solution.py:176
  607.4 30.1 %scatter_fusion.12 = f32[125,256]{1,0:T(8,128)S(1)} fusion(f32[125,256]{1,0:T(8,128)S(1)} %copy.453, s32[576]{0:T(1024)S(1)} %fusion.42, f32[576]{0:T(1024)S(1)} %pad_maximum_fusion.16), kind=kCustom, calls=%fused_computation.82 | custom fusion | flops 576 | bytes 11520 | tf_op jit(solution)/shard_map/scatter-add | solution.py:179
  677.7 40.0 %fusion.68 = f32[512]{0:T(512)S(1)} fusion(pred[512]{0:T(512)(128)(4,1)S(1)} %get-tuple-element.99, f32[512]{0:T(512)S(1)} %gather_fusion.29, pred[512]{0:T(512)(128)(4,1)S(1)} %get-tuple-element.97, pred[512]{0:T(512)(128)(4,1)S(1)} %get-tuple-element.96, pred[512]{0:T(512)(128)(4,1)S(1)} %get-tuple-element.95, pred[512]{0:T(512)(128)(4,1)S(1)} %get-tuple-element.94, ...), kind=kLoop, calls=%fused_computation.321 | loop fusion | flops 34304 | bytes 37121 | tf_op jit(solution)/shard_map/jit(_where)/select_n | solution.py:176
  717.8 30.1 %scatter_fusion.14 = f32[125,256]{1,0:T(8,128)S(1)} fusion(f32[125,256]{1,0:T(8,128)S(1)} %copy.461, s32[576]{0:T(1024)S(1)} %fusion.42, f32[576]{0:T(1024)S(1)} %pad_maximum_fusion.17), kind=kCustom, calls=%fused_computation.86 | custom fusion | flops 576 | bytes 11520 | tf_op jit(solution)/shard_map/scatter-add | solution.py:179
  787.3 40.0 %fusion.65 = f32[512]{0:T(512)S(1)} fusion(pred[512]{0:T(512)(128)(4,1)S(1)} %get-tuple-element.99, f32[512]{0:T(512)S(1)} %gather_fusion.34, pred[512]{0:T(512)(128)(4,1)S(1)} %get-tuple-element.97, pred[512]{0:T(512)(128)(4,1)S(1)} %get-tuple-element.96, pred[512]{0:T(512)(128)(4,1)S(1)} %get-tuple-element.95, pred[512]{0:T(512)(128)(4,1)S(1)} %get-tuple-element.94, ...), kind=kLoop, calls=%fused_computation.317 | loop fusion | flops 34304 | bytes 37121 | tf_op jit(solution)/shard_map/jit(_where)/select_n | solution.py:176
  827.3 30.1 %scatter_fusion.16 = f32[125,256]{1,0:T(8,128)S(1)} fusion(f32[125,256]{1,0:T(8,128)S(1)} %copy.469, s32[576]{0:T(1024)S(1)} %fusion.42, f32[576]{0:T(1024)S(1)} %pad_maximum_fusion.18), kind=kCustom, calls=%fused_computation.90 | custom fusion | flops 576 | bytes 11520 | tf_op jit(solution)/shard_map/scatter-add | solution.py:179
  897.5 40.0 %fusion.62 = f32[512]{0:T(512)S(1)} fusion(pred[512]{0:T(512)(128)(4,1)S(1)} %get-tuple-element.99, f32[512]{0:T(512)S(1)} %gather_fusion.39, pred[512]{0:T(512)(128)(4,1)S(1)} %get-tuple-element.97, pred[512]{0:T(512)(128)(4,1)S(1)} %get-tuple-element.96, pred[512]{0:T(512)(128)(4,1)S(1)} %get-tuple-element.95, pred[512]{0:T(512)(128)(4,1)S(1)} %get-tuple-element.94, ...), kind=kLoop, calls=%fused_computation.313 | loop fusion | flops 34304 | bytes 37121 | tf_op jit(solution)/shard_map/jit(_where)/select_n | solution.py:176
  937.5 30.1 %scatter_fusion.18 = f32[125,256]{1,0:T(8,128)S(1)} fusion(f32[125,256]{1,0:T(8,128)S(1)} %copy.477, s32[576]{0:T(1024)S(1)} %fusion.42, f32[576]{0:T(1024)S(1)} %pad_maximum_fusion.19), kind=kCustom, calls=%fused_computation.94 | custom fusion | flops 576 | bytes 11520 | tf_op jit(solution)/shard_map/scatter-add | solution.py:179
  1006.8 40.0 %fusion.59 = f32[512]{0:T(512)S(1)} fusion(pred[512]{0:T(512)(128)(4,1)S(1)} %get-tuple-element.99, f32[512]{0:T(512)S(1)} %gather_fusion.44, pred[512]{0:T(512)(128)(4,1)S(1)} %get-tuple-element.97, pred[512]{0:T(512)(128)(4,1)S(1)} %get-tuple-element.96, pred[512]{0:T(512)(128)(4,1)S(1)} %get-tuple-element.95, pred[512]{0:T(512)(128)(4,1)S(1)} %get-tuple-element.94, ...), kind=kLoop, calls=%fused_computation.309 | loop fusion | flops 34304 | bytes 37121 | tf_op jit(solution)/shard_map/jit(_where)/select_n | solution.py:176
  1046.9 30.1 %scatter_fusion.20 = f32[125,256]{1,0:T(8,128)S(1)} fusion(f32[125,256]{1,0:T(8,128)S(1)} %copy.485, s32[576]{0:T(1024)S(1)} %fusion.42, f32[576]{0:T(1024)S(1)} %pad_maximum_fusion.20), kind=kCustom, calls=%fused_computation.98 | custom fusion | flops 576 | bytes 11520 | tf_op jit(solution)/shard_map/scatter-add | solution.py:179
  1117.2 40.0 %fusion.56 = f32[512]{0:T(512)S(1)} fusion(pred[512]{0:T(512)(128)(4,1)S(1)} %get-tuple-element.99, f32[512]{0:T(512)S(1)} %gather_fusion.49, pred[512]{0:T(512)(128)(4,1)S(1)} %get-tuple-element.97, pred[512]{0:T(512)(128)(4,1)S(1)} %get-tuple-element.96, pred[512]{0:T(512)(128)(4,1)S(1)} %get-tuple-element.95, pred[512]{0:T(512)(128)(4,1)S(1)} %get-tuple-element.94, ...), kind=kLoop, calls=%fused_computation.305 | loop fusion | flops 34304 | bytes 37121 | tf_op jit(solution)/shard_map/jit(_where)/select_n | solution.py:176
  1157.2 30.1 %scatter_fusion.22 = f32[125,256]{1,0:T(8,128)S(1)} fusion(f32[125,256]{1,0:T(8,128)S(1)} %copy.493, s32[576]{0:T(1024)S(1)} %fusion.42, f32[576]{0:T(1024)S(1)} %pad_maximum_fusion.21), kind=kCustom, calls=%fused_computation.102 | custom fusion | flops 576 | bytes 11520 | tf_op jit(solution)/shard_map/scatter-add | solution.py:179
  1217.7 5.6 all-to-all-done.11
  1226.4 39.9 %fusion.53 = f32[512]{0:T(512)S(1)} fusion(pred[512]{0:T(512)(128)(4,1)S(1)} %get-tuple-element.99, f32[512]{0:T(512)S(1)} %gather_fusion.54, pred[512]{0:T(512)(128)(4,1)S(1)} %get-tuple-element.97, pred[512]{0:T(512)(128)(4,1)S(1)} %get-tuple-element.96, pred[512]{0:T(512)(128)(4,1)S(1)} %get-tuple-element.95, pred[512]{0:T(512)(128)(4,1)S(1)} %get-tuple-element.94, ...), kind=kLoop, calls=%fused_computation.301 | loop fusion | flops 34304 | bytes 37121 | tf_op jit(solution)/shard_map/jit(_where)/select_n | solution.py:176
  1266.2 30.1 %scatter_fusion.24 = f32[125,256]{1,0:T(8,128)S(1)} fusion(f32[125,256]{1,0:T(8,128)S(1)} %copy.501, s32[576]{0:T(1024)S(1)} %fusion.42, f32[576]{0:T(1024)S(1)} %pad_maximum_fusion.22), kind=kCustom, calls=%fused_computation.106 | custom fusion | flops 576 | bytes 11520 | tf_op jit(solution)/shard_map/scatter-add | solution.py:179
  1337.4 39.9 %fusion.50 = f32[512]{0:T(512)S(1)} fusion(pred[512]{0:T(512)(128)(4,1)S(1)} %get-tuple-element.99, f32[512]{0:T(512)S(1)} %gather_fusion.59, pred[512]{0:T(512)(128)(4,1)S(1)} %get-tuple-element.97, pred[512]{0:T(512)(128)(4,1)S(1)} %get-tuple-element.96, pred[512]{0:T(512)(128)(4,1)S(1)} %get-tuple-element.95, pred[512]{0:T(512)(128)(4,1)S(1)} %get-tuple-element.94, ...), kind=kLoop, calls=%fused_computation.297 | loop fusion | flops 34304 | bytes 37121 | tf_op jit(solution)/shard_map/jit(_where)/select_n | solution.py:176
  1377.3 30.1 %scatter_fusion.26 = f32[125,256]{1,0:T(8,128)S(1)} fusion(f32[125,256]{1,0:T(8,128)S(1)} %copy.509, s32[576]{0:T(1024)S(1)} %fusion.42, f32[576]{0:T(1024)S(1)} %pad_maximum_fusion.23), kind=kCustom, calls=%fused_computation.110 | custom fusion | flops 576 | bytes 11520 | tf_op jit(solution)/shard_map/scatter-add | solution.py:179
  (638 shorter events, 465.8 us)
Async XLA Ops:
  7.8 7.6 collective-permute-start
  8.3 7.1 collective-permute-start.3
  93.6 13.0 all-to-all-start
  112.4 12.6 all-to-all-start.1
  217.5 6.0 collective-permute-start.9
  224.2 11.0 all-to-all-start.2
  312.7 4.7 collective-permute-start.13
  328.1 5.0 collective-permute-start.14
  333.8 11.0 all-to-all-start.3
  421.9 4.6 collective-permute-start.18
  437.2 6.0 collective-permute-start.19
  444.0 11.2 all-to-all-start.4
  547.6 5.0 collective-permute-start.24
  553.3 11.0 all-to-all-start.5
  656.9 6.0 collective-permute-start.29
  663.7 11.0 all-to-all-start.6
  767.1 5.0 collective-permute-start.34
  772.8 11.4 all-to-all-start.7
  876.7 6.1 collective-permute-start.39
  883.4 11.0 all-to-all-start.8
  971.6 4.7 collective-permute-start.43
  987.0 5.0 collective-permute-start.44
  992.7 11.0 all-to-all-start.9
  1080.8 4.7 collective-permute-start.48
  1096.2 6.0 collective-permute-start.49
  1102.9 11.2 all-to-all-start.10
  1191.2 4.7 collective-permute-start.53
  1206.6 5.0 collective-permute-start.54
  1212.3 11.0 all-to-all-start.11
  1300.5 4.7 collective-permute-start.58
  1315.8 6.8 collective-permute-start.59
  1323.4 11.0 all-to-all-start.12
  (50 other events, 222.3 us)
where the time goes:
time: 1420 us; the launch traced here: 1410 us
  other arithmetic  1000 us (70%)
  local copies, waits for them, and re-layouts  181 us (13%)
  starting transfers between devices  102 us (7%)
  waiting for transfers between devices  94.7 us (7%)
  matrix products  23.8 us (2%)
    select_n x12, other arithmetic, body(): jnp.where(is_box, box_terms, 0.0)  480 us
    scatter-add x12, other arithmetic, body(): driving = driving.at[target_rows, target_cols].add(values)  362 us
    all_to_all x12, waiting for transfers between devices, body(): lax.all_to_all(crossed, 'blk', split_axis=1, concat_axis=1, tiled=True)  67.6 us
    all_to_all x12, starting transfers between devices, body(): lax.all_to_all(crossed, 'blk', split_axis=1, concat_axis=1, tiled=True)  58.6 us
    gather x12, local copies, waits for them, and re-layouts, body(): velocity[point_node, point_element]  54.2 us
    scatter-add x12, other arithmetic, body(): box_send = jnp.zeros((slot_total,), jnp.float32).at[point_column].add(jnp...  49 us
    gather x12, local copies, waits for them, and re-layouts, body(): traction = assembled[point_node, point_element]  45 us
    ppermute x60, starting transfers between devices, partner_2(): lax.ppermute(value, axis, [(i, i ^ 1 << stride) for i in range(lax.axis_s...  40.2 us
  transfers between devices with their start and end apart: 73, of which 37 were waited for; matrix products, arithmetic and copies ran while one was open for 6% of the time, Pallas kernels for 0%

commit v1 on v0

--- a/solution.py
+++ b/solution.py
@@ -8,6 +8,18 @@
 STEPS = 12
 DT_SQUARED = 0.05
 PENALTY = 10.0
+
+
+def in_blocks(x, dim, size):
+    shape = x.shape
+    parts = x.reshape(*shape[:dim], size, shape[dim] // size, *shape[dim + 1 :])
+    return jnp.moveaxis(parts, dim, 0)
+
+
+def laid_out(blocks, dim):
+    blocks = jnp.moveaxis(blocks, 0, dim)
+    dims = blocks.shape
+    return blocks.reshape(*dims[:dim], dims[dim] * dims[dim + 1], *dims[dim + 2 :])
 
 
 def partner_2(value, axis, stride):
@@ -166,7 +178,15 @@
         global_send = velocity[remote_node, remote_element] * remote_flag
         dispatch = jnp.where(is_box, box_send, global_send).reshape(CAPC, blocks)
         crossed = partner_2(dispatch, "sec", 0)
-        received = lax.all_to_all(crossed, "blk", split_axis=1, concat_axis=1, tiled=True)
+        size, position = (lax.axis_size("blk"), lax.axis_index("blk"))
+        blocks_2 = in_blocks(crossed, 1, size)
+        out = blocks_2
+        for step in range(1, size):
+            target, source = ((position + step) % size, (position - step) % size)
+            sent = lax.dynamic_index_in_dim(blocks_2, target, 0)
+            other = lax.ppermute(sent, "blk", [(i_2, (i_2 + step) % size) for i_2 in range(size)])
+            out = lax.dynamic_update_slice_in_dim(out, other, source, axis=0)
+        received = laid_out(out, 1)
         received = received.reshape(slot_total)
         remote_velocity = received[point_column]
         box_terms = jnp.where(

time: 1420 us -> 2530 us (1.78)
  waiting for transfers between devices: 94.7 us -> 495 us
  other arithmetic: 1000 us -> 1400 us
  local copies, waits for them, and re-layouts: 181 us -> 404 us
  starting transfers between devices: 102 us -> 159 us
    ppermute x0 -> x180, waiting for transfers between devices: none -> 488 us  [body(): lax.ppermute(sent, 'blk', [(i_2, (i_2 + step) % size) for i_2 in range(si...]
    scatter-add x12, other arithmetic: 362 us -> 737 us  [body(): driving = driving.at[target_rows, target_cols].add(values)]
    dynamic_update_slice x0 -> x180, local copies, waits for them, and re-layouts: none -> 187 us  [body(): out = lax.dynamic_update_slice_in_dim(out, other, source, axis=0)]
    all_to_all x12 -> x0, waiting for transfers between devices: 67.6 us -> none  [body(): lax.all_to_all(crossed, 'blk', split_axis=1, concat_axis=1, tiled=True)]
    ppermute x0 -> x180, starting transfers between devices: none -> 65.2 us  [body(): lax.ppermute(sent, 'blk', [(i_2, (i_2 + step) % size) for i_2 in range(si...]
    all_to_all x12 -> x0, starting transfers between devices: 58.6 us -> none  [body(): lax.all_to_all(crossed, 'blk', split_axis=1, concat_axis=1, tiled=True)]
    ppermute x60, starting transfers between devices: 40.2 us -> 90.2 us  [partner_2(): lax.ppermute(value, axis, [(i, i ^ 1 << stride) for i in range(lax.axis_s...]
  transfers between devices with their start and end apart: 73 -> 241, of which waited for: 37 -> 139; matrix products, arithmetic and copies ran while one was open for 6% -> 11% of each run, Pallas kernels for 0% -> 0%
where the time goes in v1:
time: 2530 us; the launch traced here: 2500 us
  other arithmetic  1400 us (55%)
  waiting for transfers between devices  495 us (20%)
  local copies, waits for them, and re-layouts  404 us (16%)
  starting transfers between devices  159 us (6%)
  matrix products  30.5 us (1%)
    scatter-add x12, other arithmetic, body(): driving = driving.at[target_rows, target_cols].add(values)  737 us
    ppermute x180, waiting for transfers between devices, body(): lax.ppermute(sent, 'blk', [(i_2, (i_2 + step) % size) for i_2 in range(si...  488 us
    select_n x12, other arithmetic, body(): jnp.where(is_box, box_terms, 0.0)  476 us
    dynamic_update_slice x180, local copies, waits for them, and re-layouts, body(): out = lax.dynamic_update_slice_in_dim(out, other, source, axis=0)  187 us
    ppermute x60, starting transfers between devices, partner_2(): lax.ppermute(value, axis, [(i, i ^ 1 << stride) for i in range(lax.axis_s...  90.2 us
    ppermute x180, starting transfers between devices, body(): lax.ppermute(sent, 'blk', [(i_2, (i_2 + step) % size) for i_2 in range(si...  65.2 us
    gather x12, local copies, waits for them, and re-layouts, body(): velocity[point_node, point_element]  54.2 us
    gather x12, local copies, waits for them, and re-layouts, body(): traction = assembled[point_node, point_element]  52.5 us
  transfers between devices with their start and end apart: 241, of which 139 were waited for; matrix products, arithmetic and copies ran while one was open for 11% of the time, Pallas kernels for 0%

profile of v1, /device:TPU:0, one launch (start us, length us, event | category | flops | bytes accessed | tf_op | source)
XLA Modules:
  0.0 2497.3 jit_solution(220404514875286184)
XLA Ops:
  29.0 22.8 scatter_fusion.1
  51.8 22.8 scatter_fusion.2
  74.5 22.8 scatter_fusion.3
  123.1 6.2 collective-permute-done.6
  173.2 39.7 %fusion.263 = (f32[512]{0:T(512)S(1)}, pred[512]{0:T(512)(128)(4,1)S(1)}, pred[512]{0:T(512)(128)(4,1)S(1)}, pred[512]{0:T(512)(128)(4,1)S(1)}, pred[512]{0:T(51...) fusion(pred[512]{0:T(512)(128)(4,1)S(1)} %get-tuple-element.99,, ...), kind=kLoop, calls=%fused_computation.701 | loop fusion | flops 66560 | bytes 39169 | tf_op jit(solution)/shard_map/jit(_where)/select_n | solution.py:196
  212.9 30.1 %scatter_fusion.4 = f32[125,256]{1,0:T(8,128)S(1)} fusion(f32[125,256]{1,0:T(8,128)S(1)} %copy.1286, s32[576]{0:T(1024)S(1)} %fusion.42, f32[576]{0:T(1024)S(1)} %pad_maximum_fusion.12), kind=kCustom, calls=%fused_computation.66 | custom fusion | flops 576 | bytes 11520 | tf_op jit(solution)/shard_map/scatter-add | solution.py:199
  276.6 5.7 collective-permute-done.25
  282.4 6.2 collective-permute-done.26
  332.2 39.6 %fusion.260 = f32[512]{0:T(512)S(1)} fusion(pred[512]{0:T(512)(128)(4,1)S(1)} %get-tuple-element.99, f32[512]{0:T(512)S(1)} %gather_fusion.9, pred[512]{0:T(512)(128)(4,1)S(1)} %get-tuple-element.97, pred[512]{0:T(512)(128)(4,1)S(1)} %get-tuple-element.96, pred[512]{0:T(512)(128)(4,1)S(1)} %get-tuple-element.95, pred[512]{0:T(512)(128)(4,1)S(1)} %get-tuple-element.94, ...), kind=kLoop, calls=%fused_computation.697 | loop fusion | flops 34304 | bytes 37121 | tf_op jit(solution)/shard_map/jit(_where)/select_n | solution.py:196
  371.9 30.1 %scatter_fusion.6 = f32[125,256]{1,0:T(8,128)S(1)} fusion(f32[125,256]{1,0:T(8,128)S(1)} %copy.1307, s32[576]{0:T(1024)S(1)} %fusion.42, f32[576]{0:T(1024)S(1)} %pad_maximum_fusion.13), kind=kCustom, calls=%fused_computation.70 | custom fusion | flops 576 | bytes 11520 | tf_op jit(solution)/shard_map/scatter-add | solution.py:199
  503.9 39.5 %fusion.257 = f32[512]{0:T(512)S(1)} fusion(pred[512]{0:T(512)(128)(4,1)S(1)} %get-tuple-element.99, f32[512]{0:T(512)S(1)} %gather_fusion.14, pred[512]{0:T(512)(128)(4,1)S(1)} %get-tuple-element.97, pred[512]{0:T(512)(128)(4,1)S(1)} %get-tuple-element.96, pred[512]{0:T(512)(128)(4,1)S(1)} %get-tuple-element.95, pred[512]{0:T(512)(128)(4,1)S(1)} %get-tuple-element.94, ...), kind=kLoop, calls=%fused_computation.693 | loop fusion | flops 34304 | bytes 37121 | tf_op jit(solution)/shard_map/jit(_where)/select_n | solution.py:196
  543.4 71.9 %scatter_fusion.8 = f32[125,256]{1,0:T(8,128)} fusion(f32[125,256]{1,0:T(8,128)} %copy.1328, s32[576]{0:T(1024)S(1)} %fusion.42, f32[576]{0:T(1024)S(1)} %pad_maximum_fusion.14), kind=kCustom, calls=%fused_computation.74 | custom fusion | flops 576 | bytes 11520 | tf_op jit(solution)/shard_map/scatter-add | solution.py:199
  718.3 39.5 %fusion.254 = f32[512]{0:T(512)S(1)} fusion(pred[512]{0:T(512)(128)(4,1)S(1)} %get-tuple-element.99, f32[512]{0:T(512)S(1)} %gather_fusion.19, pred[512]{0:T(512)(128)(4,1)S(1)} %get-tuple-element.97, pred[512]{0:T(512)(128)(4,1)S(1)} %get-tuple-element.96, pred[512]{0:T(512)(128)(4,1)S(1)} %get-tuple-element.95, pred[512]{0:T(512)(128)(4,1)S(1)} %get-tuple-element.94, ...), kind=kLoop, calls=%fused_computation.689 | loop fusion | flops 34304 | bytes 37121 | tf_op jit(solution)/shard_map/jit(_where)/select_n | solution.py:196
  757.8 71.9 %scatter_fusion.10 = f32[125,256]{1,0:T(8,128)} fusion(f32[125,256]{1,0:T(8,128)} %copy.1349, s32[576]{0:T(1024)S(1)} %fusion.42, f32[576]{0:T(1024)S(1)} %pad_maximum_fusion.15), kind=kCustom, calls=%fused_computation.78 | custom fusion | flops 576 | bytes 11520 | tf_op jit(solution)/shard_map/scatter-add | solution.py:199
  932.9 39.5 %fusion.251 = f32[512]{0:T(512)S(1)} fusion(pred[512]{0:T(512)(128)(4,1)S(1)} %get-tuple-element.99, f32[512]{0:T(512)S(1)} %gather_fusion.24, pred[512]{0:T(512)(128)(4,1)S(1)} %get-tuple-element.97, pred[512]{0:T(512)(128)(4,1)S(1)} %get-tuple-element.96, pred[512]{0:T(512)(128)(4,1)S(1)} %get-tuple-element.95, pred[512]{0:T(512)(128)(4,1)S(1)} %get-tuple-element.94, ...), kind=kLoop, calls=%fused_computation.685 | loop fusion | flops 34304 | bytes 37121 | tf_op jit(solution)/shard_map/jit(_where)/select_n | solution.py:196
  972.5 71.9 %scatter_fusion.12 = f32[125,256]{1,0:T(8,128)} fusion(f32[125,256]{1,0:T(8,128)} %copy.1370, s32[576]{0:T(1024)S(1)} %fusion.42, f32[576]{0:T(1024)S(1)} %pad_maximum_fusion.16), kind=kCustom, calls=%fused_computation.82 | custom fusion | flops 576 | bytes 11520 | tf_op jit(solution)/shard_map/scatter-add | solution.py:199
  1147.3 39.5 %fusion.248 = f32[512]{0:T(512)S(1)} fusion(pred[512]{0:T(512)(128)(4,1)S(1)} %get-tuple-element.99, f32[512]{0:T(512)S(1)} %gather_fusion.29, pred[512]{0:T(512)(128)(4,1)S(1)} %get-tuple-element.97, pred[512]{0:T(512)(128)(4,1)S(1)} %get-tuple-element.96, pred[512]{0:T(512)(128)(4,1)S(1)} %get-tuple-element.95, pred[512]{0:T(512)(128)(4,1)S(1)} %get-tuple-element.94, ...), kind=kLoop, calls=%fused_computation.681 | loop fusion | flops 34304 | bytes 37121 | tf_op jit(solution)/shard_map/jit(_where)/select_n | solution.py:196
  1186.9 71.9 %scatter_fusion.14 = f32[125,256]{1,0:T(8,128)} fusion(f32[125,256]{1,0:T(8,128)} %copy.1391, s32[576]{0:T(1024)S(1)} %fusion.42, f32[576]{0:T(1024)S(1)} %pad_maximum_fusion.17), kind=kCustom, calls=%fused_computation.86 | custom fusion | flops 576 | bytes 11520 | tf_op jit(solution)/shard_map/scatter-add | solution.py:199
  1361.8 39.7 %fusion.245 = f32[512]{0:T(512)S(1)} fusion(pred[512]{0:T(512)(128)(4,1)S(1)} %get-tuple-element.99, f32[512]{0:T(512)S(1)} %gather_fusion.34, pred[512]{0:T(512)(128)(4,1)S(1)} %get-tuple-element.97, pred[512]{0:T(512)(128)(4,1)S(1)} %get-tuple-element.96, pred[512]{0:T(512)(128)(4,1)S(1)} %get-tuple-element.95, pred[512]{0:T(512)(128)(4,1)S(1)} %get-tuple-element.94, ...), kind=kLoop, calls=%fused_computation.677 | loop fusion | flops 34304 | bytes 37121 | tf_op jit(solution)/shard_map/jit(_where)/select_n | solution.py:196
  1401.5 71.9 %scatter_fusion.16 = f32[125,256]{1,0:T(8,128)} fusion(f32[125,256]{1,0:T(8,128)} %copy.1412, s32[576]{0:T(1024)S(1)} %fusion.42, f32[576]{0:T(1024)S(1)} %pad_maximum_fusion.18), kind=kCustom, calls=%fused_computation.90 | custom fusion | flops 576 | bytes 11520 | tf_op jit(solution)/shard_map/scatter-add | solution.py:199
  1576.6 39.7 %fusion.242 = f32[512]{0:T(512)S(1)} fusion(pred[512]{0:T(512)(128)(4,1)S(1)} %get-tuple-element.99, f32[512]{0:T(512)S(1)} %gather_fusion.39, pred[512]{0:T(512)(128)(4,1)S(1)} %get-tuple-element.97, pred[512]{0:T(512)(128)(4,1)S(1)} %get-tuple-element.96, pred[512]{0:T(512)(128)(4,1)S(1)} %get-tuple-element.95, pred[512]{0:T(512)(128)(4,1)S(1)} %get-tuple-element.94, ...), kind=kLoop, calls=%fused_computation.673 | loop fusion | flops 34304 | bytes 37121 | tf_op jit(solution)/shard_map/jit(_where)/select_n | solution.py:196
  1616.2 71.9 %scatter_fusion.18 = f32[125,256]{1,0:T(8,128)} fusion(f32[125,256]{1,0:T(8,128)} %copy.1433, s32[576]{0:T(1024)S(1)} %fusion.42, f32[576]{0:T(1024)S(1)} %pad_maximum_fusion.19), kind=kCustom, calls=%fused_computation.94 | custom fusion | flops 576 | bytes 11520 | tf_op jit(solution)/shard_map/scatter-add | solution.py:199
  1791.1 39.7 %fusion.239 = f32[512]{0:T(512)S(1)} fusion(pred[512]{0:T(512)(128)(4,1)S(1)} %get-tuple-element.99, f32[512]{0:T(512)S(1)} %gather_fusion.44, pred[512]{0:T(512)(128)(4,1)S(1)} %get-tuple-element.97, pred[512]{0:T(512)(128)(4,1)S(1)} %get-tuple-element.96, pred[512]{0:T(512)(128)(4,1)S(1)} %get-tuple-element.95, pred[512]{0:T(512)(128)(4,1)S(1)} %get-tuple-element.94, ...), kind=kLoop, calls=%fused_computation.669 | loop fusion | flops 34304 | bytes 37121 | tf_op jit(solution)/shard_map/jit(_where)/select_n | solution.py:196
  1830.8 71.9 %scatter_fusion.20 = f32[125,256]{1,0:T(8,128)} fusion(f32[125,256]{1,0:T(8,128)} %copy.1454, s32[576]{0:T(1024)S(1)} %fusion.42, f32[576]{0:T(1024)S(1)} %pad_maximum_fusion.20), kind=kCustom, calls=%fused_computation.98 | custom fusion | flops 576 | bytes 11520 | tf_op jit(solution)/shard_map/scatter-add | solution.py:199
  2005.7 39.7 %fusion.236 = f32[512]{0:T(512)S(1)} fusion(pred[512]{0:T(512)(128)(4,1)S(1)} %get-tuple-element.99, f32[512]{0:T(512)S(1)} %gather_fusion.49, pred[512]{0:T(512)(128)(4,1)S(1)} %get-tuple-element.97, pred[512]{0:T(512)(128)(4,1)S(1)} %get-tuple-element.96, pred[512]{0:T(512)(128)(4,1)S(1)} %get-tuple-element.95, pred[512]{0:T(512)(128)(4,1)S(1)} %get-tuple-element.94, ...), kind=kLoop, calls=%fused_computation.665 | loop fusion | flops 34304 | bytes 37121 | tf_op jit(solution)/shard_map/jit(_where)/select_n | solution.py:196
  2045.5 71.9 %scatter_fusion.22 = f32[125,256]{1,0:T(8,128)} fusion(f32[125,256]{1,0:T(8,128)} %copy.1475, s32[576]{0:T(1024)S(1)} %fusion.42, f32[576]{0:T(1024)S(1)} %pad_maximum_fusion.21), kind=kCustom, calls=%fused_computation.102 | custom fusion | flops 576 | bytes 11520 | tf_op jit(solution)/shard_map/scatter-add | solution.py:199
  2220.4 39.8 %fusion.233 = f32[512]{0:T(512)S(1)} fusion(pred[512]{0:T(512)(128)(4,1)S(1)} %get-tuple-element.99, f32[512]{0:T(512)S(1)} %gather_fusion.54, pred[512]{0:T(512)(128)(4,1)S(1)} %get-tuple-element.97, pred[512]{0:T(512)(128)(4,1)S(1)} %get-tuple-element.96, pred[512]{0:T(512)(128)(4,1)S(1)} %get-tuple-element.95, pred[512]{0:T(512)(128)(4,1)S(1)} %get-tuple-element.94, ...), kind=kLoop, calls=%fused_computation.661 | loop fusion | flops 34304 | bytes 37121 | tf_op jit(solution)/shard_map/jit(_where)/select_n | solution.py:196
  2260.2 71.9 %scatter_fusion.24 = f32[125,256]{1,0:T(8,128)} fusion(f32[125,256]{1,0:T(8,128)} %copy.1496, s32[576]{0:T(1024)S(1)} %fusion.42, f32[576]{0:T(1024)S(1)} %pad_maximum_fusion.22), kind=kCustom, calls=%fused_computation.106 | custom fusion | flops 576 | bytes 11520 | tf_op jit(solution)/shard_map/scatter-add | solution.py:199
  2370.1 5.7 collective-permute-done.225
  2375.9 6.2 collective-permute-done.226
  2425.8 40.0 %fusion.230 = f32[512]{0:T(512)S(1)} fusion(pred[512]{0:T(512)(128)(4,1)S(1)} %get-tuple-element.99, f32[512]{0:T(512)S(1)} %gather_fusion.59, pred[512]{0:T(512)(128)(4,1)S(1)} %get-tuple-element.97, pred[512]{0:T(512)(128)(4,1)S(1)} %get-tuple-element.96, pred[512]{0:T(512)(128)(4,1)S(1)} %get-tuple-element.95, pred[512]{0:T(512)(128)(4,1)S(1)} %get-tuple-element.94, ...), kind=kLoop, calls=%fused_computation.657 | loop fusion | flops 34304 | bytes 37121 | tf_op jit(solution)/shard_map/jit(_where)/select_n | solution.py:196
  2465.9 30.1 %scatter_fusion.26 = f32[125,256]{1,0:T(8,128)S(1)} fusion(f32[125,256]{1,0:T(8,128)S(1)} %copy.1517, s32[576]{0:T(1024)S(1)} %fusion.42, f32[576]{0:T(1024)S(1)} %pad_maximum_fusion.23), kind=kCustom, calls=%fused_computation.110 | custom fusion | flops 576 | bytes 11520 | tf_op jit(solution)/shard_map/scatter-add | solution.py:199
  (1152 shorter events, 1182.0 us)
Async XLA Ops:
  113.4 56.7 %collective-permute-start.19 = (f32[1,4,1]{0,1,2:T(4,128)S(1)}, f32[1,4,1]{0,1,2:T(4,128)S(1)}, u32[]{:S(2)}, u32[]{:S(2)}) collective-permute-start(f32[1,4,1]{0,1,2:T(4,128)S(1)} %get-tuple-element.324), channel_id=1, source_target_pairs={{0,15},{1,0},{2,1},{3,2},{4,3},{5,4},{6,5},{7,6},{8,7},{9,8},{10,9... | collective-permute-start | bytes 56 | tf_op jit(solution)/shard_map/ppermute | solution.py:187
  272.3 56.9 %collective-permute-start.39 = (f32[1,4,1]{0,1,2:T(4,128)S(1)}, f32[1,4,1]{0,1,2:T(4,128)S(1)}, u32[]{:S(2)}, u32[]{:S(2)}) collective-permute-start(f32[1,4,1]{0,1,2:T(4,128)S(1)} %get-tuple-element.309), channel_id=1, source_target_pairs={{0,15},{1,0},{2,1},{3,2},{4,3},{5,4},{6,5},{7,6},{8,7},{9,8},{10,9... | collective-permute-start | bytes 56 | tf_op jit(solution)/shard_map/ppermute | solution.py:187
  272.4 56.7 %collective-permute-start.38 = (f32[1,4,1]{0,1,2:T(4,128)S(1)}, f32[1,4,1]{0,1,2:T(4,128)S(1)}, u32[]{:S(2)}, u32[]{:S(2)}) collective-permute-start(f32[1,4,1]{0,1,2:T(4,128)S(1)} %get-tuple-element.310), channel_id=1, source_target_pairs={{0,14},{1,15},{2,0},{3,1},{4,2},{5,3},{6,4},{7,5},{8,6},{9,7},{10,... | collective-permute-start | bytes 56 | tf_op jit(solution)/shard_map/ppermute | solution.py:187
  437.0 61.8 %collective-permute-start.59 = (f32[1,4,1]{0,1,2:T(4,128)S(1)}, f32[1,4,1]{0,1,2:T(4,128)S(1)}, u32[]{:S(2)}, u32[]{:S(2)}) collective-permute-start(f32[1,4,1]{0,1,2:T(4,128)S(1)} %get-tuple-element.294), channel_id=1, source_target_pairs={{0,15},{1,0},{2,1},{3,2},{4,3},{5,4},{6,5},{7,6},{8,7},{9,8},{10,9... | collective-permute-start | bytes 56 | tf_op jit(solution)/shard_map/ppermute | solution.py:187
  437.4 60.0 %collective-permute-start.58 = (f32[1,4,1]{0,1,2:T(4,128)S(1)}, f32[1,4,1]{0,1,2:T(4,128)S(1)}, u32[]{:S(2)}, u32[]{:S(2)}) collective-permute-start(f32[1,4,1]{0,1,2:T(4,128)S(1)} %get-tuple-element.295), channel_id=1, source_target_pairs={{0,14},{1,15},{2,0},{3,1},{4,2},{5,3},{6,4},{7,5},{8,6},{9,7},{10,... | collective-permute-start | bytes 56 | tf_op jit(solution)/shard_map/ppermute | solution.py:187
  438.4 57.7 %collective-permute-start.57 = (f32[1,4,1]{0,1,2:T(4,128)S(1)}, f32[1,4,1]{0,1,2:T(4,128)S(1)}, u32[]{:S(2)}, u32[]{:S(2)}) collective-permute-start(f32[1,4,1]{0,1,2:T(4,128)S(1)} %get-tuple-element.296), channel_id=1, source_target_pairs={{0,13},{1,14},{2,15},{3,0},{4,1},{5,2},{6,3},{7,4},{8,5},{9,6},{10... | collective-permute-start | bytes 56 | tf_op jit(solution)/shard_map/ppermute | solution.py:187
  651.3 61.8 %collective-permute-start.79 = (f32[1,4,1]{0,1,2:T(4,128)S(1)}, f32[1,4,1]{0,1,2:T(4,128)S(1)}, u32[]{:S(2)}, u32[]{:S(2)}) collective-permute-start(f32[1,4,1]{0,1,2:T(4,128)S(1)} %get-tuple-element.279), channel_id=1, source_target_pairs={{0,15},{1,0},{2,1},{3,2},{4,3},{5,4},{6,5},{7,6},{8,7},{9,8},{10,9... | collective-permute-start | bytes 56 | tf_op jit(solution)/shard_map/ppermute | solution.py:187
  651.7 60.1 %collective-permute-start.78 = (f32[1,4,1]{0,1,2:T(4,128)S(1)}, f32[1,4,1]{0,1,2:T(4,128)S(1)}, u32[]{:S(2)}, u32[]{:S(2)}) collective-permute-start(f32[1,4,1]{0,1,2:T(4,128)S(1)} %get-tuple-element.280), channel_id=1, source_target_pairs={{0,14},{1,15},{2,0},{3,1},{4,2},{5,3},{6,4},{7,5},{8,6},{9,7},{10,... | collective-permute-start | bytes 56 | tf_op jit(solution)/shard_map/ppermute | solution.py:187
  653.2 57.2 %collective-permute-start.77 = (f32[1,4,1]{0,1,2:T(4,128)S(1)}, f32[1,4,1]{0,1,2:T(4,128)S(1)}, u32[]{:S(2)}, u32[]{:S(2)}) collective-permute-start(f32[1,4,1]{0,1,2:T(4,128)S(1)} %get-tuple-element.281), channel_id=1, source_target_pairs={{0,13},{1,14},{2,15},{3,0},{4,1},{5,2},{6,3},{7,4},{8,5},{9,6},{10... | collective-permute-start | bytes 56 | tf_op jit(solution)/shard_map/ppermute | solution.py:187
  865.8 61.8 %collective-permute-start.99 = (f32[1,4,1]{0,1,2:T(4,128)S(1)}, f32[1,4,1]{0,1,2:T(4,128)S(1)}, u32[]{:S(2)}, u32[]{:S(2)}) collective-permute-start(f32[1,4,1]{0,1,2:T(4,128)S(1)} %get-tuple-element.264), channel_id=1, source_target_pairs={{0,15},{1,0},{2,1},{3,2},{4,3},{5,4},{6,5},{7,6},{8,7},{9,8},{10,9... | collective-permute-start | bytes 56 | tf_op jit(solution)/shard_map/ppermute | solution.py:187
  866.2 60.0 %collective-permute-start.98 = (f32[1,4,1]{0,1,2:T(4,128)S(1)}, f32[1,4,1]{0,1,2:T(4,128)S(1)}, u32[]{:S(2)}, u32[]{:S(2)}) collective-permute-start(f32[1,4,1]{0,1,2:T(4,128)S(1)} %get-tuple-element.265), channel_id=1, source_target_pairs={{0,14},{1,15},{2,0},{3,1},{4,2},{5,3},{6,4},{7,5},{8,6},{9,7},{10,... | collective-permute-start | bytes 56 | tf_op jit(solution)/shard_map/ppermute | solution.py:187
  867.6 57.2 %collective-permute-start.97 = (f32[1,4,1]{0,1,2:T(4,128)S(1)}, f32[1,4,1]{0,1,2:T(4,128)S(1)}, u32[]{:S(2)}, u32[]{:S(2)}) collective-permute-start(f32[1,4,1]{0,1,2:T(4,128)S(1)} %get-tuple-element.266), channel_id=1, source_target_pairs={{0,13},{1,14},{2,15},{3,0},{4,1},{5,2},{6,3},{7,4},{8,5},{9,6},{10... | collective-permute-start | bytes 56 | tf_op jit(solution)/shard_map/ppermute | solution.py:187
  1080.4 61.8 %collective-permute-start.119 = (f32[1,4,1]{0,1,2:T(4,128)S(1)}, f32[1,4,1]{0,1,2:T(4,128)S(1)}, u32[]{:S(2)}, u32[]{:S(2)}) collective-permute-start(f32[1,4,1]{0,1,2:T(4,128)S(1)} %get-tuple-element.249), channel_id=1, source_target_pairs={{0,15},{1,0},{2,1},{3,2},{4,3},{5,4},{6,5},{7,6},{8,7},{9,8},{10,9... | collective-permute-start | bytes 56 | tf_op jit(solution)/shard_map/ppermute | solution.py:187
  1080.7 60.2 %collective-permute-start.118 = (f32[1,4,1]{0,1,2:T(4,128)S(1)}, f32[1,4,1]{0,1,2:T(4,128)S(1)}, u32[]{:S(2)}, u32[]{:S(2)}) collective-permute-start(f32[1,4,1]{0,1,2:T(4,128)S(1)} %get-tuple-element.250), channel_id=1, source_target_pairs={{0,14},{1,15},{2,0},{3,1},{4,2},{5,3},{6,4},{7,5},{8,6},{9,7},{10,... | collective-permute-start | bytes 56 | tf_op jit(solution)/shard_map/ppermute | solution.py:187
  1082.3 57.2 %collective-permute-start.117 = (f32[1,4,1]{0,1,2:T(4,128)S(1)}, f32[1,4,1]{0,1,2:T(4,128)S(1)}, u32[]{:S(2)}, u32[]{:S(2)}) collective-permute-start(f32[1,4,1]{0,1,2:T(4,128)S(1)} %get-tuple-element.251), channel_id=1, source_target_pairs={{0,13},{1,14},{2,15},{3,0},{4,1},{5,2},{6,3},{7,4},{8,5},{9,6},{10... | collective-permute-start | bytes 56 | tf_op jit(solution)/shard_map/ppermute | solution.py:187
  1294.8 61.8 %collective-permute-start.139 = (f32[1,4,1]{0,1,2:T(4,128)S(1)}, f32[1,4,1]{0,1,2:T(4,128)S(1)}, u32[]{:S(2)}, u32[]{:S(2)}) collective-permute-start(f32[1,4,1]{0,1,2:T(4,128)S(1)} %get-tuple-element.234), channel_id=1, source_target_pairs={{0,15},{1,0},{2,1},{3,2},{4,3},{5,4},{6,5},{7,6},{8,7},{9,8},{10,9... | collective-permute-start | bytes 56 | tf_op jit(solution)/shard_map/ppermute | solution.py:187
  1295.2 60.1 %collective-permute-start.138 = (f32[1,4,1]{0,1,2:T(4,128)S(1)}, f32[1,4,1]{0,1,2:T(4,128)S(1)}, u32[]{:S(2)}, u32[]{:S(2)}) collective-permute-start(f32[1,4,1]{0,1,2:T(4,128)S(1)} %get-tuple-element.235), channel_id=1, source_target_pairs={{0,14},{1,15},{2,0},{3,1},{4,2},{5,3},{6,4},{7,5},{8,6},{9,7},{10,... | collective-permute-start | bytes 56 | tf_op jit(solution)/shard_map/ppermute | solution.py:187
  1296.7 57.2 %collective-permute-start.137 = (f32[1,4,1]{0,1,2:T(4,128)S(1)}, f32[1,4,1]{0,1,2:T(4,128)S(1)}, u32[]{:S(2)}, u32[]{:S(2)}) collective-permute-start(f32[1,4,1]{0,1,2:T(4,128)S(1)} %get-tuple-element.236), channel_id=1, source_target_pairs={{0,13},{1,14},{2,15},{3,0},{4,1},{5,2},{6,3},{7,4},{8,5},{9,6},{10... | collective-permute-start | bytes 56 | tf_op jit(solution)/shard_map/ppermute | solution.py:187
  1509.4 61.8 %collective-permute-start.159 = (f32[1,4,1]{0,1,2:T(4,128)S(1)}, f32[1,4,1]{0,1,2:T(4,128)S(1)}, u32[]{:S(2)}, u32[]{:S(2)}) collective-permute-start(f32[1,4,1]{0,1,2:T(4,128)S(1)} %get-tuple-element.219), channel_id=1, source_target_pairs={{0,15},{1,0},{2,1},{3,2},{4,3},{5,4},{6,5},{7,6},{8,7},{9,8},{10,9... | collective-permute-start | bytes 56 | tf_op jit(solution)/shard_map/ppermute | solution.py:187
  1509.8 60.0 %collective-permute-start.158 = (f32[1,4,1]{0,1,2:T(4,128)S(1)}, f32[1,4,1]{0,1,2:T(4,128)S(1)}, u32[]{:S(2)}, u32[]{:S(2)}) collective-permute-start(f32[1,4,1]{0,1,2:T(4,128)S(1)} %get-tuple-element.220), channel_id=1, source_target_pairs={{0,14},{1,15},{2,0},{3,1},{4,2},{5,3},{6,4},{7,5},{8,6},{9,7},{10,... | collective-permute-start | bytes 56 | tf_op jit(solution)/shard_map/ppermute | solution.py:187
  1511.3 57.2 %collective-permute-start.157 = (f32[1,4,1]{0,1,2:T(4,128)S(1)}, f32[1,4,1]{0,1,2:T(4,128)S(1)}, u32[]{:S(2)}, u32[]{:S(2)}) collective-permute-start(f32[1,4,1]{0,1,2:T(4,128)S(1)} %get-tuple-element.221), channel_id=1, source_target_pairs={{0,13},{1,14},{2,15},{3,0},{4,1},{5,2},{6,3},{7,4},{8,5},{9,6},{10... | collective-permute-start | bytes 56 | tf_op jit(solution)/shard_map/ppermute | solution.py:187
  1724.2 61.8 %collective-permute-start.179 = (f32[1,4,1]{0,1,2:T(4,128)S(1)}, f32[1,4,1]{0,1,2:T(4,128)S(1)}, u32[]{:S(2)}, u32[]{:S(2)}) collective-permute-start(f32[1,4,1]{0,1,2:T(4,128)S(1)} %get-tuple-element.204), channel_id=1, source_target_pairs={{0,15},{1,0},{2,1},{3,2},{4,3},{5,4},{6,5},{7,6},{8,7},{9,8},{10,9... | collective-permute-start | bytes 56 | tf_op jit(solution)/shard_map/ppermute | solution.py:187
  1724.6 60.1 %collective-permute-start.178 = (f32[1,4,1]{0,1,2:T(4,128)S(1)}, f32[1,4,1]{0,1,2:T(4,128)S(1)}, u32[]{:S(2)}, u32[]{:S(2)}) collective-permute-start(f32[1,4,1]{0,1,2:T(4,128)S(1)} %get-tuple-element.205), channel_id=1, source_target_pairs={{0,14},{1,15},{2,0},{3,1},{4,2},{5,3},{6,4},{7,5},{8,6},{9,7},{10,... | collective-permute-start | bytes 56 | tf_op jit(solution)/shard_map/ppermute | solution.py:187
  1726.1 57.2 %collective-permute-start.177 = (f32[1,4,1]{0,1,2:T(4,128)S(1)}, f32[1,4,1]{0,1,2:T(4,128)S(1)}, u32[]{:S(2)}, u32[]{:S(2)}) collective-permute-start(f32[1,4,1]{0,1,2:T(4,128)S(1)} %get-tuple-element.206), channel_id=1, source_target_pairs={{0,13},{1,14},{2,15},{3,0},{4,1},{5,2},{6,3},{7,4},{8,5},{9,6},{10... | collective-permute-start | bytes 56 | tf_op jit(solution)/shard_map/ppermute | solution.py:187
  1938.7 61.8 %collective-permute-start.199 = (f32[1,4,1]{0,1,2:T(4,128)S(1)}, f32[1,4,1]{0,1,2:T(4,128)S(1)}, u32[]{:S(2)}, u32[]{:S(2)}) collective-permute-start(f32[1,4,1]{0,1,2:T(4,128)S(1)} %get-tuple-element.189), channel_id=1, source_target_pairs={{0,15},{1,0},{2,1},{3,2},{4,3},{5,4},{6,5},{7,6},{8,7},{9,8},{10,9... | collective-permute-start | bytes 56 | tf_op jit(solution)/shard_map/ppermute | solution.py:187
  1939.2 60.0 %collective-permute-start.198 = (f32[1,4,1]{0,1,2:T(4,128)S(1)}, f32[1,4,1]{0,1,2:T(4,128)S(1)}, u32[]{:S(2)}, u32[]{:S(2)}) collective-permute-start(f32[1,4,1]{0,1,2:T(4,128)S(1)} %get-tuple-element.190), channel_id=1, source_target_pairs={{0,14},{1,15},{2,0},{3,1},{4,2},{5,3},{6,4},{7,5},{8,6},{9,7},{10,... | collective-permute-start | bytes 56 | tf_op jit(solution)/shard_map/ppermute | solution.py:187
  1940.6 57.2 %collective-permute-start.197 = (f32[1,4,1]{0,1,2:T(4,128)S(1)}, f32[1,4,1]{0,1,2:T(4,128)S(1)}, u32[]{:S(2)}, u32[]{:S(2)}) collective-permute-start(f32[1,4,1]{0,1,2:T(4,128)S(1)} %get-tuple-element.191), channel_id=1, source_target_pairs={{0,13},{1,14},{2,15},{3,0},{4,1},{5,2},{6,3},{7,4},{8,5},{9,6},{10... | collective-permute-start | bytes 56 | tf_op jit(solution)/shard_map/ppermute | solution.py:187
  2153.4 61.8 %collective-permute-start.219 = (f32[1,4,1]{0,1,2:T(4,128)S(1)}, f32[1,4,1]{0,1,2:T(4,128)S(1)}, u32[]{:S(2)}, u32[]{:S(2)}) collective-permute-start(f32[1,4,1]{0,1,2:T(4,128)S(1)} %get-tuple-element.174), channel_id=1, source_target_pairs={{0,15},{1,0},{2,1},{3,2},{4,3},{5,4},{6,5},{7,6},{8,7},{9,8},{10,9... | collective-permute-start | bytes 56 | tf_op jit(solution)/shard_map/ppermute | solution.py:187
  2153.8 60.0 %collective-permute-start.218 = (f32[1,4,1]{0,1,2:T(4,128)S(1)}, f32[1,4,1]{0,1,2:T(4,128)S(1)}, u32[]{:S(2)}, u32[]{:S(2)}) collective-permute-start(f32[1,4,1]{0,1,2:T(4,128)S(1)} %get-tuple-element.175), channel_id=1, source_target_pairs={{0,14},{1,15},{2,0},{3,1},{4,2},{5,3},{6,4},{7,5},{8,6},{9,7},{10,... | collective-permute-start | bytes 56 | tf_op jit(solution)/shard_map/ppermute | solution.py:187
  2155.3 57.2 %collective-permute-start.217 = (f32[1,4,1]{0,1,2:T(4,128)S(1)}, f32[1,4,1]{0,1,2:T(4,128)S(1)}, u32[]{:S(2)}, u32[]{:S(2)}) collective-permute-start(f32[1,4,1]{0,1,2:T(4,128)S(1)} %get-tuple-element.176), channel_id=1, source_target_pairs={{0,13},{1,14},{2,15},{3,0},{4,1},{5,2},{6,3},{7,4},{8,5},{9,6},{10... | collective-permute-start | bytes 56 | tf_op jit(solution)/shard_map/ppermute | solution.py:187
  2365.9 56.9 %collective-permute-start.239 = (f32[1,4,1]{0,1,2:T(4,128)S(1)}, f32[1,4,1]{0,1,2:T(4,128)S(1)}, u32[]{:S(2)}, u32[]{:S(2)}) collective-permute-start(f32[1,4,1]{0,1,2:T(4,128)S(1)} %get-tuple-element.159), channel_id=1, source_target_pairs={{0,15},{1,0},{2,1},{3,2},{4,3},{5,4},{6,5},{7,6},{8,7},{9,8},{10,9... | collective-permute-start | bytes 56 | tf_op jit(solution)/shard_map/ppermute | solution.py:187
  2365.9 56.7 %collective-permute-start.238 = (f32[1,4,1]{0,1,2:T(4,128)S(1)}, f32[1,4,1]{0,1,2:T(4,128)S(1)}, u32[]{:S(2)}, u32[]{:S(2)}) collective-permute-start(f32[1,4,1]{0,1,2:T(4,128)S(1)} %get-tuple-element.160), channel_id=1, source_target_pairs={{0,14},{1,15},{2,0},{3,1},{4,2},{5,3},{6,4},{7,5},{8,6},{9,7},{10,... | collective-permute-start | bytes 56 | tf_op jit(solution)/shard_map/ppermute | solution.py:187
  (223 other events, 3014.8 us)
